TPU v7x, 32 devices: a whole 2x2x4 slice. The times are simulated.
32 devices in a mesh: groups: 2 (over x), depth: 16 (over z, y, core).
Axes of the slice: x: 2, y: 2, z: 4, core: 2. Of those that a mesh axis runs over, the one named last changes fastest.
Arguments:
- fields: float32 [32, 2, 2, 512, 256], P(('groups', 'depth')), parts along dimension 0, may hold values from -6 to 6
- vel_tiles: float32 [64, 128, 128], P(('groups', 'depth')), parts along dimension 0, may hold values from 0.5 to 2
- tile_ids: int32 [32, 2, 4, 2], P(('groups', 'depth')), parts along dimension 0, may hold values from 0 to 31
- orders: int32 [32, 2], P(('groups', 'depth')), parts along dimension 0, may hold values from 1 to 3
- term_weights: float32 [3], replicated, may hold values from 0.05 to 0.12
- phase_rates: float32 [4], replicated, may hold values from 1 to 4
- owners: int32 [32, 16], P(('groups', 'depth')), parts along dimension 0, may hold values from 0 to 15, as said below
- image_slots: int32 [32, 16], P(('groups', 'depth')), parts along dimension 0, may hold values from 0 to 7
Outputs:
- image_volume: float32 [256, 128, 128], P(('groups', 'depth')), parts along dimension 0
- wavefields_out: float32 [32, 2, 2, 512, 256], P(('groups', 'depth')), parts along dimension 0
There are 2 independent parts, one for each index of `groups`. A program takes and returns all parts, laid end to end along the dimension named above; an argument that names none is the same for every part. Nothing has to cross between parts.
Inputs may be any that keep to these rules, and one draw needn't show every extreme that they name: `owners`: of the 16 tiles of one slab, at most 2 have the same owner, and some owner gets exactly 2 of them.
All inputs are finite; a program needn't handle non-finite values.
Results may differ from a plain program's by a relative error of at most 0.0003.
Values sent between devices are 32-bit elements; how exact they have to be, the bound alone decides.
A program may use at most 64 MiB of HBM per device.

v0:
```python
import jax
import jax.numpy as jnp
from jax import lax
from jax.experimental import pallas as pl
from jax.experimental.pallas import tpu as pltpu
from jax.sharding import PartitionSpec as P

TICKS = 2
CAP = 2
IMG_SLOTS = 8
LANES = 128
HALO = 8
ROWS = 32
VMEM = pltpu.VMEM
SMEM = pltpu.SMEM


def specs(*spaces):
    return [pl.BlockSpec(memory_space=space) for space in spaces]


def from_behind(shard, axis, by):
    peers = lax.axis_size(axis)
    pairs = [(i, i + by) for i in range(peers) if 0 <= i + by < peers]
    return lax.ppermute(shard, axis, pairs)


def sincos(angle):
    turns = jnp.floor(angle * 0.6366197723675814 + 0.5)
    quarter = turns.astype(jnp.int32)
    r = angle - turns * 1.5703125
    r = r - turns * 4.837512969970703e-4
    r = r - turns * 7.54978995489188e-8
    r2 = r * r
    s = r + r * r2 * (-1.6666654611e-1 + r2 * (8.3321608736e-3 - r2 * 1.9515295891e-4))
    c = 1.0 - 0.5 * r2 + r2 * r2 * (
        4.166664568298827e-2 + r2 * (-1.388731625493765e-3 + r2 * 2.443315711809948e-5)
    )
    odd = (quarter & 1) == 1
    sin_out = jnp.where(odd, c, s)
    cos_out = jnp.where(odd, s, c)
    sin_out = jnp.where((quarter & 2) == 2, -sin_out, sin_out)
    cos_out = jnp.where(((quarter + 1) & 2) == 2, -cos_out, cos_out)
    return sin_out, cos_out


def table_kernel(ids_ref, orders_ref, term_ref, rates_ref, library_ref, table_ref):
    _, steps, tiles_x, tiles_y = ids_ref.shape
    degrees = rates_ref.shape[0]
    tile = library_ref.shape[1]
    zeroth = 1.0 - sum(term_ref[k] for k in range(degrees - 1))
    for j in range(steps):
        order = orders_ref[0, j]
        weights = [zeroth] + [
            jnp.where(order >= k, term_ref[k - 1], 0.0) for k in range(1, degrees)
        ]
        for b in range(tiles_y):
            for a in range(tiles_x):
                source = ids_ref[0, j, a, b]

                def body(i, _):
                    r0 = pl.multiple_of(i * ROWS, ROWS)
                    slow = library_ref[source, pl.ds(r0, ROWS), :]
                    for k in range(degrees):
                        sin_now, cos_now = sincos(rates_ref[k] * slow)
                        rows = pl.ds(a * tile + r0, ROWS)
                        table_ref[j, k, 0, b, rows, :] = weights[k] * cos_now
                        table_ref[j, k, 1, b, rows, :] = weights[k] * sin_now
                    return 0

                lax.fori_loop(0, tile // ROWS, body, 0)


def smooth(ref, f, halves, r0, lane):
    centre, down = [], []
    for h in range(halves):
        c = ref[f, h, pl.ds(r0 + HALO, ROWS), :]
        u = ref[f, h, pl.ds(r0 + HALO - 1, ROWS), :]
        d = ref[f, h, pl.ds(r0 + HALO + 1, ROWS), :]
        centre.append(c)
        down.append((u + d) + (c + c))
    right = [pltpu.roll(v, 1, 1) for v in down]
    left = [pltpu.roll(v, LANES - 1, 1) for v in down]
    out = []
    for h in range(halves):
        before = jnp.where(lane == 0, right[h - 1] if h else 0.0, right[h])
        after = jnp.where(lane == LANES - 1, left[h + 1] if h + 1 < halves else 0.0, left[h])
        out.append((before + after) + (down[h] + down[h]))
    return out, centre


def clear_halos(refs, halves, rows):
    zero = jnp.zeros((HALO, LANES), jnp.float32)
    for ref in refs:
        for f in range(2):
            for h in range(halves):
                ref[f, h, 0:HALO, :] = zero
                ref[f, h, rows + HALO : rows + 2 * HALO, :] = zero


def load_state(state_ref, p0, halves, rows):
    def body(i, _):
        r0 = pl.multiple_of(i * ROWS, ROWS)
        for f in range(2):
            for h in range(halves):
                p0[f, h, pl.ds(r0 + HALO, ROWS), :] = state_ref[
                    f, pl.ds(r0, ROWS), h * LANES : (h + 1) * LANES
                ]
        return 0

    lax.fori_loop(0, rows // ROWS, body, 0)


def depth_step(table_ref, j, sign, p0, p1, p2, halves, rows, emit):
    lane = lax.broadcasted_iota(jnp.int32, (ROWS, LANES), 1)
    chunks = rows // ROWS

    def first(i, _):
        r0 = pl.multiple_of(i * ROWS, ROWS)
        for f in range(2):
            soft, centre = smooth(p0, f, halves, r0, lane)
            for h in range(halves):
                p1[f, h, pl.ds(r0 + HALO, ROWS), :] = 0.125 * soft[h] - centre[h]
        return 0

    def second(i, _):
        r0 = pl.multiple_of(i * ROWS, ROWS)
        for f in range(2):
            soft, centre = smooth(p1, f, halves, r0, lane)
            for h in range(halves):
                here = pl.ds(r0 + HALO, ROWS)
                p2[f, h, here, :] = 0.25 * soft[h] - 2.0 * centre[h] - p0[f, h, here, :]
        return 0

    def third(i, _):
        r0 = pl.multiple_of(i * ROWS, ROWS)
        here = pl.ds(r0 + HALO, ROWS)
        terms = []
        for f in range(2):
            soft, centre = smooth(p2, f, halves, r0, lane)
            terms.append((soft, centre))
        for h in range(halves):
            series = []
            for f in range(2):
                soft, centre = terms[f]
                t0 = p0[f, h, here, :]
                t1 = p1[f, h, here, :]
                series.append((t0, t1, centre[h], 0.25 * soft[h] - 2.0 * centre[h] - t1))
            real = imag = None
            for k in range(4):
                a = table_ref[j, k, 0, h, pl.ds(r0, ROWS), :]
                b = table_ref[j, k, 1, h, pl.ds(r0, ROWS), :]
                re, im = series[0][k], series[1][k]
                if sign > 0:
                    new_real, new_imag = a * re - b * im, a * im + b * re
                else:
                    new_real, new_imag = a * re + b * im, a * im - b * re
                real = new_real if real is None else real + new_real
                imag = new_imag if imag is None else imag + new_imag
            p0[0, h, here, :] = real
            p0[1, h, here, :] = imag
            emit(j, h, r0, real, imag)
        return 0

    lax.fori_loop(0, chunks, first, 0)
    lax.fori_loop(0, chunks, second, 0)
    lax.fori_loop(0, chunks, third, 0)


def source_kernel(table_ref, state_ref, out_ref, p0, p1, p2):
    halves, rows = table_ref.shape[3], table_ref.shape[4]
    clear_halos((p0, p1, p2), halves, rows)
    load_state(state_ref, p0, halves, rows)

    def emit(j, h, r0, real, imag):
        columns = slice(h * LANES, (h + 1) * LANES)
        out_ref[j, 0, pl.ds(r0, ROWS), columns] = real
        out_ref[j, 1, pl.ds(r0, ROWS), columns] = imag

    for j in range(table_ref.shape[0]):
        depth_step(table_ref, j, 1.0, p0, p1, p2, halves, rows, emit)


def receiver_kernel(table_ref, state_ref, steps_ref, out_ref, corr_ref, p0, p1, p2):
    halves, rows = table_ref.shape[3], table_ref.shape[4]
    clear_halos((p0, p1, p2), halves, rows)
    load_state(state_ref, p0, halves, rows)
    last = table_ref.shape[0] - 1

    def emit(j, h, r0, real, imag):
        columns = slice(h * LANES, (h + 1) * LANES)
        here = pl.ds(r0, ROWS)
        if j == last:
            out_ref[0, here, columns] = real
            out_ref[1, here, columns] = imag
        corr_ref[j, h, here, :] = (
            steps_ref[j, 0, here, columns] * real + steps_ref[j, 1, here, columns] * imag
        )

    for j in range(last + 1):
        depth_step(table_ref, j, -1.0, p0, p1, p2, halves, rows, emit)


def final_kernel(
    owners_ref, slots_ref, table_ref, state_ref, steps_ref, before_ref,
    wave_ref, buffer_ref, corr, p0, p1, p2,
):
    halves, rows = table_ref.shape[3], table_ref.shape[4]
    clear_halos((p0, p1, p2), halves, rows)
    load_state(state_ref, p0, halves, rows)
    steps = table_ref.shape[0]
    last = steps - 1
    tile = LANES
    tiles_x = rows // tile

    def emit(j, h, r0, real, imag):
        columns = slice(h * LANES, (h + 1) * LANES)
        here = pl.ds(r0, ROWS)
        src_real = steps_ref[j, 0, here, columns]
        src_imag = steps_ref[j, 1, here, columns]
        if j == last:
            wave_ref[0, 0, 0, here, columns] = src_real
            wave_ref[0, 0, 1, here, columns] = src_imag
            wave_ref[0, 1, 0, here, columns] = real
            wave_ref[0, 1, 1, here, columns] = imag
        corr[j, h, here, :] = before_ref[j, h, here, :] + (src_real * real + src_imag * imag)

    for j in range(steps):
        depth_step(table_ref, j, -1.0, p0, p1, p2, halves, rows, emit)

    peers = buffer_ref.shape[0]

    def clear(o, _):
        buffer_ref[o] = jnp.zeros(buffer_ref.shape[1:], jnp.float32)
        buffer_ref[o, CAP * tile : CAP * tile + CAP, :] = jnp.full((CAP, LANES), -1.0, jnp.float32)
        return 0

    lax.fori_loop(0, peers, clear, 0)
    pieces = owners_ref.shape[1]

    for p in range(pieces):
        owner = owners_ref[0, p]
        rank = 0
        for q in range(p):
            rank = rank + jnp.where(owners_ref[0, q] == owner, 1, 0)
        j, rest = divmod(p, tiles_x * halves)
        a, h = divmod(rest, halves)
        buffer_ref[owner, pl.ds(pl.multiple_of(rank * tile, tile), tile), :] = corr[
            j, h, a * tile : (a + 1) * tile, :
        ]
        slot = slots_ref[0, p].astype(jnp.float32)
        buffer_ref[owner, pl.ds(CAP * tile + rank, 1), :] = jnp.full((1, LANES), slot, jnp.float32)


def volume_kernel(received_ref, volume_ref):
    peers = received_ref.shape[0]
    tile = volume_ref.shape[1]
    step = 16

    def body(i, _):
        r0 = pl.multiple_of(i * step, step)

        def add(peer, sums):
            sums = list(sums)
            for c in range(CAP):
                slot = received_ref[peer, CAP * tile + c : CAP * tile + c + 1, :]
                slot = jnp.broadcast_to(slot, (step, LANES))
                piece = received_ref[peer, pl.ds(c * tile + r0, step), :]
                for m in range(IMG_SLOTS):
                    sums[m] = sums[m] + jnp.where(slot == m, piece, 0.0)
            return tuple(sums)

        zero = jnp.zeros((step, LANES), jnp.float32)
        sums = lax.fori_loop(0, peers, add, (zero,) * IMG_SLOTS)
        for m in range(IMG_SLOTS):
            volume_ref[m, pl.ds(r0, step), :] = sums[m]
        return 0

    lax.fori_loop(0, tile // step, body, 0)


def local(fields, vel_tiles, tile_ids, orders, term_weights, phase_rates, owners, image_slots):
    rows, columns = fields.shape[3:]
    tile = vel_tiles.shape[1]
    steps = tile_ids.shape[1]
    degrees = phase_rates.shape[0]
    halves = columns // LANES
    peers = lax.axis_size("depth")
    f32 = jnp.float32

    def shape(*dims):
        return jax.ShapeDtypeStruct(dims, f32)

    cost = pl.CostEstimate(flops=40_000_000, bytes_accessed=14_000_000, transcendentals=0)
    padded = [VMEM((2, halves, rows + 2 * HALO, LANES), f32)] * 3

    library = lax.all_gather(vel_tiles, "depth", axis=0, tiled=True)
    table = pl.pallas_call(
        table_kernel,
        out_shape=shape(steps, degrees, 2, halves, rows, LANES),
        in_specs=specs(SMEM, SMEM, SMEM, SMEM, VMEM),
        out_specs=specs(VMEM)[0],
        name="table",
    )(tile_ids, orders, term_weights, phase_rates, library)

    source_call = pl.pallas_call(
        source_kernel,
        out_shape=shape(steps, 2, rows, columns),
        in_specs=specs(VMEM, VMEM),
        out_specs=specs(VMEM)[0],
        scratch_shapes=padded,
        cost_estimate=cost,
        name="source_step",
    )
    receiver_call = pl.pallas_call(
        receiver_kernel,
        out_shape=(shape(2, rows, columns), shape(steps, halves, rows, LANES)),
        in_specs=specs(VMEM, VMEM, VMEM),
        out_specs=specs(VMEM, VMEM),
        scratch_shapes=padded,
        cost_estimate=cost,
        name="receiver_step",
    )
    final_call = pl.pallas_call(
        final_kernel,
        out_shape=(
            shape(1, 2, 2, rows, columns),
            shape(peers, CAP * tile + HALO, LANES),
        ),
        in_specs=specs(SMEM, SMEM, VMEM, VMEM, VMEM, VMEM),
        out_specs=specs(VMEM, VMEM),
        scratch_shapes=[VMEM((steps, halves, rows, LANES), f32)] + padded,
        cost_estimate=cost,
        name="final_step",
    )

    source_steps = source_call(table, fields[0, 0])
    source = from_behind(source_steps[steps - 1], "depth", 1)
    receiver, correlation = receiver_call(table, fields[0, 1], source_steps)
    receiver = from_behind(receiver, "depth", 1)
    source_steps = source_call(table, source)
    wave, buffer = final_call(owners, image_slots, table, receiver, source_steps, correlation)
    received = lax.all_to_all(buffer, "depth", split_axis=0, concat_axis=0, tiled=True)
    volume = pl.pallas_call(
        volume_kernel,
        out_shape=shape(IMG_SLOTS, tile, LANES),
        in_specs=specs(VMEM),
        out_specs=specs(VMEM)[0],
        name="volume",
    )(received)
    return volume, wave


def solution(mesh):
    whole = P(("groups", "depth"))
    placed = (whole, whole, whole, whole, P(), P(), whole, whole)
    return jax.shard_map(
        local, mesh=mesh, in_specs=placed, out_specs=(whole, whole), check_vma=False
    )
```

profile of v0, /device:TPU:13, one launch (start us, length us, event | category | flops | bytes accessed | tf_op | source)
XLA Modules:
  0.0 203.6 jit_solution(7682161692524861230)
XLA Ops:
  7.2 0.0 all-gather.2.cloned.1.call-start
  7.2 0.7 all-gather.2.cloned.1.call-update
  7.9 1.4 copy.11.ids_ref
  9.3 3.0 %slice_bitcast_fusion.1 = (f32[2,512,256]{2,1,0:T(8,128)}, f32[2,512,256]{2,1,0:T(8,128)}) fusion(f32[1,2,2,512,256]{4,3,2,1,0:T(8,128)} %param.8), kind=kLoop, calls=%fused_computation.1 | loop fusion | bytes 4194304 | tf_op jit(solution)/shard_map/squeeze | solution.py:337
  12.2 38.9 %all-gather.2.cloned.1.call-done.library_ref = f32[32,128,128]{2,1,0:T(8,128)} async-done(((f32[2,128,128]{2,1,0:T(8,128)}), f32[32,128,128]{2,1,0:T(8,128)}) %all-gather.2.cloned.1.call-update) | async-done | bytes 2097168 | tf_op jit(solution)/shard_map/all_gather | solution.py:297
  51.2 11.3 %table.1.table_ref = f32[2,4,2,2,512,128]{5,4,3,2,1,0:T(8,128)} custom-call(s32[1,2,4,2]{3,2,1,0:T(4,128)} %copy.11.ids_ref, s32[1,2]{1,0:T(1,128)} %orders_ref.1, f32[3]{0:T(128)} %term_ref.1, f32[4]{0:T(128)} %rates_ref.1, f32[32,128,128]{2,1,0:T(8,128)} %all-gather.2.cloned.1.call-done.library_ref), custom_call_target="tpu_custom_call" | custom-call | tf_op jit(solution)/shard_map/table/pallas_call | solution.py:298
  62.5 15.9 %source_step.2.steps_ref = f32[2,2,512,256]{3,2,1,0:T(8,128)} custom-call(f32[2,4,2,2,512,128]{5,4,3,2,1,0:T(8,128)} %table.1.table_ref, f32[2,512,256]{2,1,0:T(8,128)} %get-tuple-element.10.state_ref), custom_call_target="tpu_custom_call" | custom-call | flops 40000000 | bytes 14000000 | tf_op jit(solution)/shard_map/source_step/pallas_call | solution.py:337
  78.4 1.3 slice_bitcast_fusion
  79.7 3.4 %collective-permute-start.1 = (f32[2,512,256]{2,1,0:T(8,128)S(1)}, f32[2,512,256]{2,1,0:T(8,128)S(1)}, u32[]{:S(2)}, u32[]{:S(2)}) collective-permute-start(f32[2,512,256]{2,1,0:T(8,128)S(1)} %slice_bitcast_fusion), channel_id=1, source_target_pairs={{0,1},{1,2},{2,3},{3,4},{4,5},{5,6},{6,7},{7,8},{8,9},{9,10},{10,1... | collective-permute-start | bytes 3145736 | tf_op jit(solution)/shard_map/ppermute | solution.py:25
  83.1 16.8 %receiver_step.1 = (f32[2,512,256]{2,1,0:T(8,128)}, f32[2,2,512,128]{3,2,1,0:T(8,128)}) custom-call(f32[2,4,2,2,512,128]{5,4,3,2,1,0:T(8,128)} %table.1.table_ref, f32[2,512,256]{2,1,0:T(8,128)} %get-tuple-element.11.state_ref, f32[2,2,512,256]{3,2,1,0:T(8,128)} %source_step.2.steps_ref), custom_call_target="tpu_custom_call" | custom-call | flops 40000000 | bytes 14000000 | tf_op jit(solution)/shard_map/receiver_step/pallas_call | solution.py:339
  99.9 2.1 %collective-permute-start = (f32[2,512,256]{2,1,0:T(8,128)}, f32[2,512,256]{2,1,0:T(8,128)S(1)}, u32[]{:S(2)}, u32[]{:S(2)}) collective-permute-start(f32[2,512,256]{2,1,0:T(8,128)} %get-tuple-element.6), channel_id=1, source_target_pairs={{0,1},{1,2},{2,3},{3,4},{4,5},{5,6},{6,7},{7,8},{8,9},{9,10},{10,1... | collective-permute-start | bytes 3145736 | tf_op jit(solution)/shard_map/ppermute | solution.py:25
  102.0 0.0 collective-permute-done.1.state_ref
  102.0 0.0 copy-start.1
  102.0 1.0 copy-done.1
  103.0 15.9 %source_step.3.steps_ref = f32[2,2,512,256]{3,2,1,0:T(8,128)} custom-call(f32[2,4,2,2,512,128]{5,4,3,2,1,0:T(8,128)} %table.1.table_ref, f32[2,512,256]{2,1,0:T(8,128)} %copy-done.1), custom_call_target="tpu_custom_call" | custom-call | flops 40000000 | bytes 14000000 | tf_op jit(solution)/shard_map/source_step/pallas_call | solution.py:341
  118.9 0.0 collective-permute-done.state_ref
  118.9 0.0 copy-start
  118.9 1.0 copy-done
  119.9 18.1 %final_step.1 = (f32[1,2,2,512,256]{4,3,2,1,0:T(8,128)}, f32[16,264,128]{2,1,0:T(8,128)}) custom-call(s32[1,16]{1,0:T(1,128)} %owners_ref.1, s32[1,16]{1,0:T(1,128)} %slots_ref.1, f32[2,4,2,2,512,128]{5,4,3,2,1,0:T(8,128)} %table.1.table_ref, f32[2,512,256]{2,1,0:T(8,128)} %copy-done, f32[2,2,512,256]{3,2,1,0:T(8,128)} %source_step.3.steps_ref, ...), custom_call_target="tpu_custom_call" | custom-call | flops 40000000 | bytes 14000000 | tf_op jit(solution)/shard_map/final_step/pallas_call | solution.py:342
  138.0 54.5 %all_to_all.5.received_ref = f32[16,264,128]{2,1,0:T(8,128)} all-to-all(f32[16,264,128]{2,1,0:T(8,128)} %get-tuple-element.8), channel_id=1, replica_groups=mesh['groups'=2,'depth'=16] {'depth'}, dimensions={0} | all-to-all | bytes 4325376 | tf_op jit(solution)/shard_map/all_to_all | solution.py:343
  192.5 4.3 %volume.1 = f32[8,128,128]{2,1,0:T(8,128)} custom-call(f32[16,264,128]{2,1,0:T(8,128)} %all_to_all.5.received_ref), custom_call_target="tpu_custom_call" | custom-call | tf_op jit(solution)/shard_map/volume/pallas_call | solution.py:344
Async XLA Ops:
  7.2 44.0 %all-gather.2.cloned.1.call-start = ((), (), s32[]{:S(2)}) async-start(), calls=%async_computation.1 | async-start | bytes 2228224 | tf_op jit(solution)/shard_map/all_gather | solution.py:297
  79.7 22.3 %collective-permute-start.1 = (f32[2,512,256]{2,1,0:T(8,128)S(1)}, f32[2,512,256]{2,1,0:T(8,128)S(1)}, u32[]{:S(2)}, u32[]{:S(2)}) collective-permute-start(f32[2,512,256]{2,1,0:T(8,128)S(1)} %slice_bitcast_fusion), channel_id=1, source_target_pairs={{0,1},{1,2},{2,3},{3,4},{4,5},{5,6},{6,7},{7,8},{8,9},{9,10},{10,1... | collective-permute-start | bytes 3145736 | tf_op jit(solution)/shard_map/ppermute | solution.py:25
  99.9 19.0 %collective-permute-start = (f32[2,512,256]{2,1,0:T(8,128)}, f32[2,512,256]{2,1,0:T(8,128)S(1)}, u32[]{:S(2)}, u32[]{:S(2)}) collective-permute-start(f32[2,512,256]{2,1,0:T(8,128)} %get-tuple-element.6), channel_id=1, source_target_pairs={{0,1},{1,2},{2,3},{3,4},{4,5},{5,6},{6,7},{7,8},{8,9},{9,10},{10,1... | collective-permute-start | bytes 3145736 | tf_op jit(solution)/shard_map/ppermute | solution.py:25
  102.0 1.0 copy-start.1
  118.9 1.0 copy-start
Sparse Core Ops, SparseCore 0:
  10.1 40.9 all-gather.1
where the time goes:
time: 207 us; the launch traced here: 204 us
  Pallas kernels  82.3 us (40%)
  blocking collectives  54.5 us (26%)
  waiting for transfers between devices  39.6 us (19%)
  between operations  14.1 us (7%)
  local copies, waits for them, and re-layouts  7.57 us (4%)
  starting transfers between devices  5.6 us (3%)
    all_to_all x1, blocking collectives, local(): lax.all_to_all(buffer, 'depth', split_axis=0, concat_axis=0, tiled=True)  54.5 us
    all_gather x1, waiting for transfers between devices, local(): library = lax.all_gather(vel_tiles, 'depth', axis=0, tiled=True)  38.9 us
    pallas_call x1, Pallas kernels, local(): final_call(owners, image_slots, table, receiver, source_steps, correlation)  18.1 us
    pallas_call x1, Pallas kernels, local(): receiver, correlation = receiver_call(table, fields[0, 1], source_steps)  16.8 us
    pallas_call x1, Pallas kernels, local(): source_steps = source_call(table, source)  15.9 us
    pallas_call x1, Pallas kernels, local(): source_steps = source_call(table, fields[0, 0])  15.9 us
    pallas_call x1, Pallas kernels, local(): pl.pallas_call(table_kernel, out_shape=shape(steps, degrees, 2, halves, r...  11.3 us
    ppermute x2, starting transfers between devices, from_behind(): return lax.ppermute(shard, axis, pairs)  5.56 us
  transfers between devices with their start and end apart: 3, of which 1 were waited for; matrix products, arithmetic and copies ran while one was open for 2% of the time, Pallas kernels for 16%

commit v1 on v0

--- a/solution.py
+++ b/solution.py
@@ -167,21 +167,23 @@
     lax.fori_loop(0, chunks, third, 0)
 
 
-def source_kernel(table_ref, state_ref, out_ref, p0, p1, p2):
+def source_kernel(table_ref, state_ref, out_ref, end_ref, p0, p1, p2):
     halves, rows = table_ref.shape[3], table_ref.shape[4]
     clear_halos((p0, p1, p2), halves, rows)
     load_state(state_ref, p0, halves, rows)
 
     def emit(j, h, r0, real, imag):
         columns = slice(h * LANES, (h + 1) * LANES)
-        out_ref[j, 0, pl.ds(r0, ROWS), columns] = real
-        out_ref[j, 1, pl.ds(r0, ROWS), columns] = imag
+        here = pl.ds(r0, ROWS)
+        target = end_ref if j == table_ref.shape[0] - 1 else out_ref.at[j]
+        target[0, here, columns] = real
+        target[1, here, columns] = imag
 
     for j in range(table_ref.shape[0]):
         depth_step(table_ref, j, 1.0, p0, p1, p2, halves, rows, emit)
 
 
-def receiver_kernel(table_ref, state_ref, steps_ref, out_ref, corr_ref, p0, p1, p2):
+def receiver_kernel(table_ref, state_ref, steps_ref, end_ref, out_ref, corr_ref, p0, p1, p2):
     halves, rows = table_ref.shape[3], table_ref.shape[4]
     clear_halos((p0, p1, p2), halves, rows)
     load_state(state_ref, p0, halves, rows)
@@ -193,16 +195,15 @@
         if j == last:
             out_ref[0, here, columns] = real
             out_ref[1, here, columns] = imag
-        corr_ref[j, h, here, :] = (
-            steps_ref[j, 0, here, columns] * real + steps_ref[j, 1, here, columns] * imag
-        )
+        source = end_ref if j == last else steps_ref.at[j]
+        corr_ref[j, h, here, :] = source[0, here, columns] * real + source[1, here, columns] * imag
 
     for j in range(last + 1):
         depth_step(table_ref, j, -1.0, p0, p1, p2, halves, rows, emit)
 
 
 def final_kernel(
-    owners_ref, slots_ref, table_ref, state_ref, steps_ref, before_ref,
+    owners_ref, slots_ref, table_ref, state_ref, steps_ref, end_ref, before_ref,
     wave_ref, buffer_ref, corr, p0, p1, p2,
 ):
     halves, rows = table_ref.shape[3], table_ref.shape[4]
@@ -216,8 +217,9 @@
     def emit(j, h, r0, real, imag):
         columns = slice(h * LANES, (h + 1) * LANES)
         here = pl.ds(r0, ROWS)
-        src_real = steps_ref[j, 0, here, columns]
-        src_imag = steps_ref[j, 1, here, columns]
+        source = end_ref if j == last else steps_ref.at[j]
+        src_real = source[0, here, columns]
+        src_imag = source[1, here, columns]
         if j == last:
             wave_ref[0, 0, 0, here, columns] = src_real
             wave_ref[0, 0, 1, here, columns] = src_imag
@@ -252,31 +254,129 @@
         buffer_ref[owner, pl.ds(CAP * tile + rank, 1), :] = jnp.full((1, LANES), slot, jnp.float32)
 
 
-def volume_kernel(received_ref, volume_ref):
-    peers = received_ref.shape[0]
+def remote(src, dst, send_sem, recv_sem, peer):
+    return pltpu.make_async_remote_copy(
+        src_ref=src, dst_ref=dst, send_sem=send_sem, recv_sem=recv_sem,
+        device_id={"depth": peer}, device_id_type=pl.DeviceIdType.MESH,
+    )
+
+
+def meet(peers):
+    barrier = pltpu.get_barrier_semaphore()
+    for peer in peers:
+        pl.semaphore_signal(
+            barrier, inc=1, device_id={"depth": peer}, device_id_type=pl.DeviceIdType.MESH
+        )
+    pl.semaphore_wait(barrier, len(peers))
+
+
+def gather_kernel(own_ref, library_ref, send_sem, recv_sem):
+    me = lax.axis_index("depth")
+    planes = library_ref.shape[0] // 4
+    within = me % 4
+    plane = me // 4
+    core = me % 2
+    pair = (me // 2) % 2
+
+    def at(steps):
+        return ((plane + steps + planes) % planes) * 4 + within
+
+    beside = plane * 4 + (1 - pair) * 2 + core
+    twin = me + 1 - 2 * core
+    above, below = at(1), at(-1)
+    meet([above, below, beside, twin])
+    sent = []
+
+    def send(block, peer):
+        src = own_ref if block is me else library_ref.at[block]
+        n = len(sent)
+        copy = remote(src, library_ref.at[block], send_sem.at[n], recv_sem.at[block], peer)
+        copy.start()
+        sent.append(copy)
+
+    def arrive(block):
+        remote(own_ref, library_ref.at[block], send_sem.at[0], recv_sem.at[block], twin).wait_recv()
+
+    up = planes // 2
+    down = planes - 1 - up
+    if up > 0:
+        send(me, above)
+    if down > 0:
+        send(me, below)
+    send(me, beside)
+    send(me, twin)
+    library_ref[me] = own_ref[...]
+    order = [0]
+    for step in range(1, up + 1):
+        block = at(-step)
+        order.append(-step)
+        arrive(block)
+        if step < up:
+            send(block, above)
+        send(block, beside)
+        send(block, twin)
+        if step <= down:
+            block = at(step)
+            order.append(step)
+            arrive(block)
+            if step < down:
+                send(block, below)
+            send(block, beside)
+            send(block, twin)
+    shift = (1 - 2 * pair) * 2
+    for step in order:
+        block = at(step) + shift
+        arrive(block)
+        send(block, twin)
+    flip = 1 - 2 * core
+    for step in order:
+        arrive(at(step) + flip)
+        arrive(at(step) + shift + flip)
+    for copy in sent:
+        copy.wait_send()
+
+
+def volume_kernel(buffer_ref, volume_ref, received, send_sem, recv_sem):
+    me = lax.axis_index("depth")
+    peers = buffer_ref.shape[0]
     tile = volume_ref.shape[1]
-    step = 16
-
-    def body(i, _):
-        r0 = pl.multiple_of(i * step, step)
-
-        def add(peer, sums):
-            sums = list(sums)
-            for c in range(CAP):
-                slot = received_ref[peer, CAP * tile + c : CAP * tile + c + 1, :]
-                slot = jnp.broadcast_to(slot, (step, LANES))
-                piece = received_ref[peer, pl.ds(c * tile + r0, step), :]
+    step = 32
+    meet([(me + d) % peers for d in range(1, peers)])
+    copies = []
+    for d in range(1, peers):
+        to = (me + d) % peers
+        copy = remote(buffer_ref.at[to], received.at[d], send_sem.at[d], recv_sem.at[d], to)
+        copy.start()
+        copies.append(copy)
+
+    def clear(m, _):
+        volume_ref[m] = jnp.zeros((tile, LANES), jnp.float32)
+        return 0
+
+    lax.fori_loop(0, volume_ref.shape[0], clear, 0)
+
+    def add_from(ref, block):
+        for c in range(CAP):
+            slot = ref[block, CAP * tile + c : CAP * tile + c + 1, :]
+            slot = jnp.broadcast_to(slot, (8, LANES))
+            slot = jnp.concatenate([slot] * (step // 8), axis=0)
+
+            def body(i, _):
+                r0 = pl.multiple_of(i * step, step)
+                piece = ref[block, pl.ds(c * tile + r0, step), :]
                 for m in range(IMG_SLOTS):
-                    sums[m] = sums[m] + jnp.where(slot == m, piece, 0.0)
-            return tuple(sums)
-
-        zero = jnp.zeros((step, LANES), jnp.float32)
-        sums = lax.fori_loop(0, peers, add, (zero,) * IMG_SLOTS)
-        for m in range(IMG_SLOTS):
-            volume_ref[m, pl.ds(r0, step), :] = sums[m]
-        return 0
-
-    lax.fori_loop(0, tile // step, body, 0)
+                    here = pl.ds(r0, step)
+                    volume_ref[m, here, :] += jnp.where(slot == m, piece, 0.0)
+                return 0
+
+            lax.fori_loop(0, tile // step, body, 0)
+
+    add_from(buffer_ref, me)
+    for d, copy in enumerate(copies, 1):
+        copy.wait_recv()
+        add_from(received, d)
+    for copy in copies:
+        copy.wait_send()
 
 
 def local(fields, vel_tiles, tile_ids, orders, term_weights, phase_rates, owners, image_slots):
@@ -294,7 +394,15 @@
     cost = pl.CostEstimate(flops=40_000_000, bytes_accessed=14_000_000, transcendentals=0)
     padded = [VMEM((2, halves, rows + 2 * HALO, LANES), f32)] * 3
 
-    library = lax.all_gather(vel_tiles, "depth", axis=0, tiled=True)
+    library = pl.pallas_call(
+        gather_kernel,
+        out_shape=shape(peers, *vel_tiles.shape),
+        in_specs=specs(VMEM),
+        out_specs=specs(VMEM)[0],
+        scratch_shapes=[pltpu.SemaphoreType.DMA((peers,)), pltpu.SemaphoreType.DMA((peers,))],
+        compiler_params=pltpu.CompilerParams(collective_id=0, has_side_effects=True),
+        name="gather",
+    )(vel_tiles).reshape(peers * vel_tiles.shape[0], tile, tile)
     table = pl.pallas_call(
         table_kernel,
         out_shape=shape(steps, degrees, 2, halves, rows, LANES),
@@ -303,51 +411,60 @@
         name="table",
     )(tile_ids, orders, term_weights, phase_rates, library)
 
-    source_call = pl.pallas_call(
-        source_kernel,
-        out_shape=shape(steps, 2, rows, columns),
-        in_specs=specs(VMEM, VMEM),
-        out_specs=specs(VMEM)[0],
-        scratch_shapes=padded,
-        cost_estimate=cost,
-        name="source_step",
-    )
-    receiver_call = pl.pallas_call(
+    def half_of(which):
+        return pl.BlockSpec(
+            (None, None, 2, rows, columns), lambda i: (0, which, 0, 0, 0), memory_space=VMEM
+        )
+
+    def source_call(state, spec):
+        return pl.pallas_call(
+            source_kernel,
+            grid=(1,),
+            out_shape=(shape(max(steps - 1, 1), 2, rows, columns), shape(2, rows, columns)),
+            in_specs=specs(VMEM) + [spec],
+            out_specs=specs(VMEM, VMEM),
+            scratch_shapes=padded,
+            cost_estimate=cost,
+            name="source_step",
+        )(table, state)
+
+    early, end = source_call(fields, half_of(0))
+    source = from_behind(end, "depth", 1)
+    receiver, correlation = pl.pallas_call(
         receiver_kernel,
+        grid=(1,),
         out_shape=(shape(2, rows, columns), shape(steps, halves, rows, LANES)),
-        in_specs=specs(VMEM, VMEM, VMEM),
+        in_specs=specs(VMEM) + [half_of(1)] + specs(VMEM, VMEM),
         out_specs=specs(VMEM, VMEM),
         scratch_shapes=padded,
         cost_estimate=cost,
         name="receiver_step",
-    )
-    final_call = pl.pallas_call(
+    )(table, fields, early, end)
+    receiver = from_behind(receiver, "depth", 1)
+    early, end = source_call(source, specs(VMEM)[0])
+    block_rows = CAP * tile + HALO
+    wave, buffer = pl.pallas_call(
         final_kernel,
-        out_shape=(
-            shape(1, 2, 2, rows, columns),
-            shape(peers, CAP * tile + HALO, LANES),
-        ),
-        in_specs=specs(SMEM, SMEM, VMEM, VMEM, VMEM, VMEM),
+        out_shape=(shape(1, 2, 2, rows, columns), shape(peers, block_rows, LANES)),
+        in_specs=specs(SMEM, SMEM, VMEM, VMEM, VMEM, VMEM, VMEM),
         out_specs=specs(VMEM, VMEM),
         scratch_shapes=[VMEM((steps, halves, rows, LANES), f32)] + padded,
         cost_estimate=cost,
         name="final_step",
-    )
-
-    source_steps = source_call(table, fields[0, 0])
-    source = from_behind(source_steps[steps - 1], "depth", 1)
-    receiver, correlation = receiver_call(table, fields[0, 1], source_steps)
-    receiver = from_behind(receiver, "depth", 1)
-    source_steps = source_call(table, source)
-    wave, buffer = final_call(owners, image_slots, table, receiver, source_steps, correlation)
-    received = lax.all_to_all(buffer, "depth", split_axis=0, concat_axis=0, tiled=True)
+    )(owners, image_slots, table, receiver, early, end, correlation)
     volume = pl.pallas_call(
         volume_kernel,
         out_shape=shape(IMG_SLOTS, tile, LANES),
         in_specs=specs(VMEM),
         out_specs=specs(VMEM)[0],
+        scratch_shapes=[
+            VMEM((peers, block_rows, LANES), f32),
+            pltpu.SemaphoreType.DMA((peers,)),
+            pltpu.SemaphoreType.DMA((peers,)),
+        ],
+        compiler_params=pltpu.CompilerParams(collective_id=1, has_side_effects=True),
         name="volume",
-    )(received)
+    )(buffer)
     return volume, wave
 
 

time: 207 us -> 164 us (0.79); the launches traced: 204 us -> 164 us
  Pallas kernels: 82.3 us -> 152 us
  blocking collectives: 54.5 us -> 0 us
  waiting for transfers between devices: 39.6 us -> 0.01 us
  between operations: 14.1 us -> 0.68 us
  local copies, waits for them, and re-layouts: 7.57 us -> 5.17 us
    all_to_all x1 -> x0, blocking collectives: 54.5 us -> none  [local(): lax.all_to_all(buffer, 'depth', split_axis=0, concat_axis=0, tiled=True)]
    pallas_call x1, Pallas kernels: 4.33 us -> 53.7 us  [local(): pl.pallas_call(volume_kernel, out_shape=shape(IMG_SLOTS, tile, LANES), in...]
    all_gather x1 -> x0, waiting for transfers between devices: 38.9 us -> none  [local(): library = lax.all_gather(vel_tiles, 'depth', axis=0, tiled=True)]
    pallas_call x4 -> x5, Pallas kernels: 66.6 us -> 86.8 us  [the longest x2 31.7 us: source_call(): pl.pallas_call(source_kernel, grid=(1,), out_shape=(shape(max(steps - 1,...]
    squeeze x2 -> x0, local copies, waits for them, and re-layouts: 4.27 us -> none  [the longest x1 2.97 us: local(): source_steps = source_call(table, fields[0, 0])]
    unnamed x5 -> x6, local copies, waits for them, and re-layouts: 3.31 us -> 5.17 us
  transfers between devices with their start and end apart: 3 -> 2, of which waited for: 1 -> 0; matrix products, arithmetic and copies ran while one was open for 2% -> 0% of each run, Pallas kernels for 16% -> 20%
where the time goes in v1:
time: 164 us
  Pallas kernels  152 us (93%)
  starting transfers between devices  5.95 us (4%)
  local copies, waits for them, and re-layouts  5.17 us (3%)
    pallas_call x1, Pallas kernels, local(): pl.pallas_call(volume_kernel, out_shape=shape(IMG_SLOTS, tile, LANES), in...  53.7 us
    pallas_call x2, Pallas kernels, source_call(): pl.pallas_call(source_kernel, grid=(1,), out_shape=(shape(max(steps - 1,...  31.7 us
    pallas_call x1, Pallas kernels, local(): pl.pallas_call(gather_kernel, out_shape=shape(peers, *vel_tiles.shape), i...  20.4 us
    pallas_call x1, Pallas kernels, local(): pl.pallas_call(final_kernel, out_shape=(shape(1, 2, 2, rows, columns), sh...  18.1 us
    pallas_call x1, Pallas kernels, local(): pl.pallas_call(receiver_kernel, grid=(1,), out_shape=(shape(2, rows, colu...  16.6 us
    pallas_call x1, Pallas kernels, local(): pl.pallas_call(table_kernel, out_shape=shape(steps, degrees, 2, halves, r...  11.3 us
    ppermute x2, starting transfers between devices, from_behind(): return lax.ppermute(shard, axis, pairs)  5.95 us
    unnamed x6, local copies, waits for them, and re-layouts  5.17 us
  transfers between devices with their start and end apart: 2, of which 0 were waited for; matrix products, arithmetic and copies ran while one was open for 0% of the time, Pallas kernels for 20%

profile of v1, /device:TPU:13, one launch (start us, length us, event | category | flops | bytes accessed | tf_op | source)
XLA Modules:
  0.0 163.7 jit_solution(10879770178128425408)
XLA Ops:
  0.6 1.4 copy.10.ids_ref
  2.0 20.4 %gather.1 = f32[16,2,128,128]{3,2,1,0:T(8,128)} custom-call(f32[2,128,128]{2,1,0:T(8,128)} %own_ref.1), custom_call_target="tpu_custom_call" | custom-call | tf_op jit(solution)/shard_map/gather/pallas_call | solution.py:397
  22.4 11.3 %table.1.table_ref = f32[2,4,2,2,512,128]{5,4,3,2,1,0:T(8,128)} custom-call(s32[1,2,4,2]{3,2,1,0:T(4,128)} %copy.10.ids_ref, s32[1,2]{1,0:T(1,128)} %orders_ref.1, f32[3]{0:T(128)} %term_ref.1, f32[4]{0:T(128)} %rates_ref.1, f32[32,128,128]{2,1,0:T(8,128)} %bitcast.1), custom_call_target="tpu_custom_call" | custom-call | tf_op jit(solution)/shard_map/table/pallas_call | solution.py:406
  33.8 15.8 %source_step.2 = (f32[1,2,512,256]{3,2,1,0:T(8,128)}, f32[2,512,256]{2,1,0:T(8,128)}) custom-call(f32[2,4,2,2,512,128]{5,4,3,2,1,0:T(8,128)} %table.1.table_ref, f32[1,2,2,512,256]{4,3,2,1,0:T(8,128)} %state_ref.3), custom_call_target="tpu_custom_call" | custom-call | flops 40000000 | bytes 14000000 | tf_op jit(solution)/shard_map/source_step/pallas_call | solution.py:420
  49.5 3.7 %collective-permute-start.1 = (f32[2,512,256]{2,1,0:T(8,128)}, f32[2,512,256]{2,1,0:T(8,128)S(1)}, u32[]{:S(2)}, u32[]{:S(2)}) collective-permute-start(f32[2,512,256]{2,1,0:T(8,128)} %get-tuple-element.11.end_ref), channel_id=1, source_target_pairs={{0,1},{1,2},{2,3},{3,4},{4,5},{5,6},{6,7},{7,8},{8,9},{9,10},{10,1... | collective-permute-start | bytes 3145736 | tf_op jit(solution)/shard_map/ppermute | solution.py:25
  53.2 16.6 %receiver_step.1 = (f32[2,512,256]{2,1,0:T(8,128)}, f32[2,2,512,128]{3,2,1,0:T(8,128)}) custom-call(f32[2,4,2,2,512,128]{5,4,3,2,1,0:T(8,128)} %table.1.table_ref, f32[1,2,2,512,256]{4,3,2,1,0:T(8,128)} %state_ref.3, f32[1,2,512,256]{3,2,1,0:T(8,128)} %get-tuple-element.10.steps_ref, f32[2,512,256]{2,1,0:T(8,128)} %get-tuple-element.11.end_ref), custom_call_target="tpu_custom_call" | custom-call | flops 40000000 | bytes 14000000 | tf_op jit(solution)/shard_map/receiver_step/pallas_call | solution.py:433
  69.9 2.3 %collective-permute-start = (f32[2,512,256]{2,1,0:T(8,128)}, f32[2,512,256]{2,1,0:T(8,128)S(1)}, u32[]{:S(2)}, u32[]{:S(2)}) collective-permute-start(f32[2,512,256]{2,1,0:T(8,128)} %get-tuple-element.12), channel_id=1, source_target_pairs={{0,1},{1,2},{2,3},{3,4},{4,5},{5,6},{6,7},{7,8},{8,9},{9,10},{10,1... | collective-permute-start | bytes 3145736 | tf_op jit(solution)/shard_map/ppermute | solution.py:25
  72.1 0.0 collective-permute-done.1.state_ref
  72.2 0.0 copy-start.1
  72.2 1.0 copy-done.1
  73.1 15.9 %source_step.3 = (f32[1,2,512,256]{3,2,1,0:T(8,128)}, f32[2,512,256]{2,1,0:T(8,128)}) custom-call(f32[2,4,2,2,512,128]{5,4,3,2,1,0:T(8,128)} %table.1.table_ref, f32[2,512,256]{2,1,0:T(8,128)} %copy-done.1), custom_call_target="tpu_custom_call" | custom-call | flops 40000000 | bytes 14000000 | tf_op jit(solution)/shard_map/source_step/pallas_call | solution.py:420
  89.0 0.0 collective-permute-done.state_ref
  89.0 0.0 copy-start
  89.0 1.0 copy-done
  90.0 18.1 %final_step.1 = (f32[1,2,2,512,256]{4,3,2,1,0:T(8,128)}, f32[16,264,128]{2,1,0:T(8,128)}) custom-call(s32[1,16]{1,0:T(1,128)} %owners_ref.1, s32[1,16]{1,0:T(1,128)} %slots_ref.1, f32[2,4,2,2,512,128]{5,4,3,2,1,0:T(8,128)} %table.1.table_ref, f32[2,512,256]{2,1,0:T(8,128)} %copy-done, f32[1,2,512,256]{3,2,1,0:T(8,128)} %get-tuple-element.13.steps_ref, ...), custom_call_target="tpu_custom_call" | custom-call | flops 40000000 | bytes 14000000 | tf_op jit(solution)/shard_map/final_step/pallas_call | solution.py:446
  108.1 53.7 %volume.1 = f32[8,128,128]{2,1,0:T(8,128)} custom-call(f32[16,264,128]{2,1,0:T(8,128)} %get-tuple-element.16.buffer_ref), custom_call_target="tpu_custom_call" | custom-call | tf_op jit(solution)/shard_map/volume/pallas_call | solution.py:455
  161.9 1.9 %copy.12 = f32[8,128,128]{2,1,0:T(8,128)} copy(f32[8,128,128]{2,1,0:T(8,128)} %volume.1) | data formatting | bytes 1048576
Async XLA Ops:
  49.5 22.6 %collective-permute-start.1 = (f32[2,512,256]{2,1,0:T(8,128)}, f32[2,512,256]{2,1,0:T(8,128)S(1)}, u32[]{:S(2)}, u32[]{:S(2)}) collective-permute-start(f32[2,512,256]{2,1,0:T(8,128)} %get-tuple-element.11.end_ref), channel_id=1, source_target_pairs={{0,1},{1,2},{2,3},{3,4},{4,5},{5,6},{6,7},{7,8},{8,9},{9,10},{10,1... | collective-permute-start | bytes 3145736 | tf_op jit(solution)/shard_map/ppermute | solution.py:25
  69.9 19.2 %collective-permute-start = (f32[2,512,256]{2,1,0:T(8,128)}, f32[2,512,256]{2,1,0:T(8,128)S(1)}, u32[]{:S(2)}, u32[]{:S(2)}) collective-permute-start(f32[2,512,256]{2,1,0:T(8,128)} %get-tuple-element.12), channel_id=1, source_target_pairs={{0,1},{1,2},{2,3},{3,4},{4,5},{5,6},{6,7},{7,8},{8,9},{9,10},{10,1... | collective-permute-start | bytes 3145736 | tf_op jit(solution)/shard_map/ppermute | solution.py:25
  72.2 1.0 copy-start.1
  89.0 1.0 copy-start

commit v2 on v1

--- a/solution.py
+++ b/solution.py
@@ -29,8 +29,7 @@
     turns = jnp.floor(angle * 0.6366197723675814 + 0.5)
     quarter = turns.astype(jnp.int32)
     r = angle - turns * 1.5703125
-    r = r - turns * 4.837512969970703e-4
-    r = r - turns * 7.54978995489188e-8
+    r = r - turns * 4.838267948966192e-4
     r2 = r * r
     s = r + r * r2 * (-1.6666654611e-1 + r2 * (8.3321608736e-3 - r2 * 1.9515295891e-4))
     c = 1.0 - 0.5 * r2 + r2 * r2 * (
@@ -111,7 +110,17 @@
     lax.fori_loop(0, rows // ROWS, body, 0)
 
 
-def depth_step(table_ref, j, sign, p0, p1, p2, halves, rows, emit):
+def fetch(table_ref, table, sems):
+    copies = [
+        pltpu.make_async_copy(table_ref.at[j], table.at[j], sems.at[j])
+        for j in range(table_ref.shape[0])
+    ]
+    for copy in copies:
+        copy.start()
+    return copies
+
+
+def depth_step(table_ref, copy, j, sign, p0, p1, p2, halves, rows, emit):
     lane = lax.broadcasted_iota(jnp.int32, (ROWS, LANES), 1)
     chunks = rows // ROWS
 
@@ -162,12 +171,14 @@
             emit(j, h, r0, real, imag)
         return 0
 
-    lax.fori_loop(0, chunks, first, 0)
-    lax.fori_loop(0, chunks, second, 0)
+    lax.fori_loop(0, chunks, first, 0, unroll=2)
+    lax.fori_loop(0, chunks, second, 0, unroll=2)
+    copy.wait()
     lax.fori_loop(0, chunks, third, 0)
 
 
-def source_kernel(table_ref, state_ref, out_ref, end_ref, p0, p1, p2):
+def source_kernel(table_ref, state_ref, out_ref, end_ref, p0, p1, p2, table, sems):
+    copies = fetch(table_ref, table, sems)
     halves, rows = table_ref.shape[3], table_ref.shape[4]
     clear_halos((p0, p1, p2), halves, rows)
     load_state(state_ref, p0, halves, rows)
@@ -180,10 +191,11 @@
         target[1, here, columns] = imag
 
     for j in range(table_ref.shape[0]):
-        depth_step(table_ref, j, 1.0, p0, p1, p2, halves, rows, emit)
-
-
-def receiver_kernel(table_ref, state_ref, steps_ref, end_ref, out_ref, corr_ref, p0, p1, p2):
+        depth_step(table, copies[j], j, 1.0, p0, p1, p2, halves, rows, emit)
+
+
+def receiver_kernel(table_ref, state_ref, steps_ref, end_ref, out_ref, corr_ref, p0, p1, p2, table, sems):
+    copies = fetch(table_ref, table, sems)
     halves, rows = table_ref.shape[3], table_ref.shape[4]
     clear_halos((p0, p1, p2), halves, rows)
     load_state(state_ref, p0, halves, rows)
@@ -199,13 +211,14 @@
         corr_ref[j, h, here, :] = source[0, here, columns] * real + source[1, here, columns] * imag
 
     for j in range(last + 1):
-        depth_step(table_ref, j, -1.0, p0, p1, p2, halves, rows, emit)
+        depth_step(table, copies[j], j, -1.0, p0, p1, p2, halves, rows, emit)
 
 
 def final_kernel(
     owners_ref, slots_ref, table_ref, state_ref, steps_ref, end_ref, before_ref,
-    wave_ref, buffer_ref, corr, p0, p1, p2,
+    wave_ref, buffer_ref, corr, p0, p1, p2, table, sems,
 ):
+    copies = fetch(table_ref, table, sems)
     halves, rows = table_ref.shape[3], table_ref.shape[4]
     clear_halos((p0, p1, p2), halves, rows)
     load_state(state_ref, p0, halves, rows)
@@ -228,7 +241,7 @@
         corr[j, h, here, :] = before_ref[j, h, here, :] + (src_real * real + src_imag * imag)
 
     for j in range(steps):
-        depth_step(table_ref, j, -1.0, p0, p1, p2, halves, rows, emit)
+        depth_step(table, copies[j], j, -1.0, p0, p1, p2, halves, rows, emit)
 
     peers = buffer_ref.shape[0]
 
@@ -392,7 +405,10 @@
         return jax.ShapeDtypeStruct(dims, f32)
 
     cost = pl.CostEstimate(flops=40_000_000, bytes_accessed=14_000_000, transcendentals=0)
-    padded = [VMEM((2, halves, rows + 2 * HALO, LANES), f32)] * 3
+    padded = [VMEM((2, halves, rows + 2 * HALO, LANES), f32)] * 3 + [
+        VMEM((steps, degrees, 2, halves, rows, LANES), f32),
+        pltpu.SemaphoreType.DMA((steps,)),
+    ]
 
     library = pl.pallas_call(
         gather_kernel,
@@ -421,7 +437,7 @@
             source_kernel,
             grid=(1,),
             out_shape=(shape(max(steps - 1, 1), 2, rows, columns), shape(2, rows, columns)),
-            in_specs=specs(VMEM) + [spec],
+            in_specs=specs(pl.ANY) + [spec],
             out_specs=specs(VMEM, VMEM),
             scratch_shapes=padded,
             cost_estimate=cost,
@@ -434,7 +450,7 @@
         receiver_kernel,
         grid=(1,),
         out_shape=(shape(2, rows, columns), shape(steps, halves, rows, LANES)),
-        in_specs=specs(VMEM) + [half_of(1)] + specs(VMEM, VMEM),
+        in_specs=specs(pl.ANY) + [half_of(1)] + specs(VMEM, VMEM),
         out_specs=specs(VMEM, VMEM),
         scratch_shapes=padded,
         cost_estimate=cost,
@@ -446,7 +462,7 @@
     wave, buffer = pl.pallas_call(
         final_kernel,
         out_shape=(shape(1, 2, 2, rows, columns), shape(peers, block_rows, LANES)),
-        in_specs=specs(SMEM, SMEM, VMEM, VMEM, VMEM, VMEM, VMEM),
+        in_specs=specs(SMEM, SMEM, pl.ANY, VMEM, VMEM, VMEM, VMEM),
         out_specs=specs(VMEM, VMEM),
         scratch_shapes=[VMEM((steps, halves, rows, LANES), f32)] + padded,
         cost_estimate=cost,

time: 164 us -> 146 us (0.89)
  Pallas kernels: 152 us -> 134 us
    pallas_call x2, Pallas kernels: 31.7 us -> 22 us  [source_call(): pl.pallas_call(source_kernel, grid=(1,), out_shape=(shape(max(steps - 1,...]
    pallas_call x1, Pallas kernels: 18.1 us -> 13.3 us  [local(): pl.pallas_call(final_kernel, out_shape=(shape(1, 2, 2, rows, columns), sh...]
    pallas_call x1, Pallas kernels: 16.6 us -> 11.9 us  [local(): pl.pallas_call(receiver_kernel, grid=(1,), out_shape=(shape(2, rows, colu...]
  transfers between devices with their start and end apart: 2 -> 2, of which waited for: 0 -> 0; matrix products, arithmetic and copies ran while one was open for 0% -> 0% of each run, Pallas kernels for 20% -> 16%
where the time goes in v2:
time: 146 us
  Pallas kernels  134 us (92%)
  starting transfers between devices  5.98 us (4%)
  local copies, waits for them, and re-layouts  5.16 us (4%)
    pallas_call x1, Pallas kernels, local(): pl.pallas_call(volume_kernel, out_shape=shape(IMG_SLOTS, tile, LANES), in...  55.1 us
    pallas_call x2, Pallas kernels, source_call(): pl.pallas_call(source_kernel, grid=(1,), out_shape=(shape(max(steps - 1,...  22 us
    pallas_call x1, Pallas kernels, local(): pl.pallas_call(gather_kernel, out_shape=shape(peers, *vel_tiles.shape), i...  20.4 us
    pallas_call x1, Pallas kernels, local(): pl.pallas_call(final_kernel, out_shape=(shape(1, 2, 2, rows, columns), sh...  13.3 us
    pallas_call x1, Pallas kernels, local(): pl.pallas_call(receiver_kernel, grid=(1,), out_shape=(shape(2, rows, colu...  11.9 us
    pallas_call x1, Pallas kernels, local(): pl.pallas_call(table_kernel, out_shape=shape(steps, degrees, 2, halves, r...  11.1 us
    ppermute x2, starting transfers between devices, from_behind(): return lax.ppermute(shard, axis, pairs)  5.98 us
    unnamed x6, local copies, waits for them, and re-layouts  5.16 us
  transfers between devices with their start and end apart: 2, of which 0 were waited for; matrix products, arithmetic and copies ran while one was open for 0% of the time, Pallas kernels for 16%

profile of v2, /device:TPU:13, one launch (start us, length us, event | category | flops | bytes accessed | tf_op | source)
XLA Modules:
  0.0 145.7 jit_solution(6278861021307200282)
XLA Ops:
  0.6 1.4 copy.10.ids_ref
  2.0 20.4 %gather.1 = f32[16,2,128,128]{3,2,1,0:T(8,128)} custom-call(f32[2,128,128]{2,1,0:T(8,128)} %own_ref.1), custom_call_target="tpu_custom_call" | custom-call | tf_op jit(solution)/shard_map/gather/pallas_call | solution.py:413
  22.4 11.1 %table.1.table_ref = f32[2,4,2,2,512,128]{5,4,3,2,1,0:T(8,128)} custom-call(s32[1,2,4,2]{3,2,1,0:T(4,128)} %copy.10.ids_ref, s32[1,2]{1,0:T(1,128)} %orders_ref.1, f32[3]{0:T(128)} %term_ref.1, f32[4]{0:T(128)} %rates_ref.1, f32[32,128,128]{2,1,0:T(8,128)} %bitcast.1), custom_call_target="tpu_custom_call" | custom-call | tf_op jit(solution)/shard_map/table/pallas_call | solution.py:422
  33.5 11.0 %source_step.2 = (f32[1,2,512,256]{3,2,1,0:T(8,128)}, f32[2,512,256]{2,1,0:T(8,128)}) custom-call(f32[2,4,2,2,512,128]{5,4,3,2,1,0:T(8,128)} %table.1.table_ref, f32[1,2,2,512,256]{4,3,2,1,0:T(8,128)} %state_ref.3), custom_call_target="tpu_custom_call" | custom-call | flops 40000000 | bytes 14000000 | tf_op jit(solution)/shard_map/source_step/pallas_call | solution.py:436
  44.5 3.7 %collective-permute-start.1 = (f32[2,512,256]{2,1,0:T(8,128)}, f32[2,512,256]{2,1,0:T(8,128)S(1)}, u32[]{:S(2)}, u32[]{:S(2)}) collective-permute-start(f32[2,512,256]{2,1,0:T(8,128)} %get-tuple-element.11.end_ref), channel_id=1, source_target_pairs={{0,1},{1,2},{2,3},{3,4},{4,5},{5,6},{6,7},{7,8},{8,9},{9,10},{10,1... | collective-permute-start | bytes 3145736 | tf_op jit(solution)/shard_map/ppermute | solution.py:25
  48.1 11.9 %receiver_step.1 = (f32[2,512,256]{2,1,0:T(8,128)}, f32[2,2,512,128]{3,2,1,0:T(8,128)}) custom-call(f32[2,4,2,2,512,128]{5,4,3,2,1,0:T(8,128)} %table.1.table_ref, f32[1,2,2,512,256]{4,3,2,1,0:T(8,128)} %state_ref.3, f32[1,2,512,256]{3,2,1,0:T(8,128)} %get-tuple-element.10.steps_ref, f32[2,512,256]{2,1,0:T(8,128)} %get-tuple-element.11.end_ref), custom_call_target="tpu_custom_call" | custom-call | flops 40000000 | bytes 14000000 | tf_op jit(solution)/shard_map/receiver_step/pallas_call | solution.py:449
  60.0 2.3 %collective-permute-start = (f32[2,512,256]{2,1,0:T(8,128)}, f32[2,512,256]{2,1,0:T(8,128)S(1)}, u32[]{:S(2)}, u32[]{:S(2)}) collective-permute-start(f32[2,512,256]{2,1,0:T(8,128)} %get-tuple-element.12), channel_id=1, source_target_pairs={{0,1},{1,2},{2,3},{3,4},{4,5},{5,6},{6,7},{7,8},{8,9},{9,10},{10,1... | collective-permute-start | bytes 3145736 | tf_op jit(solution)/shard_map/ppermute | solution.py:25
  62.3 0.0 collective-permute-done.1.state_ref
  62.3 0.0 copy-start.1
  62.3 1.0 copy-done.1
  63.3 11.1 %source_step.3 = (f32[1,2,512,256]{3,2,1,0:T(8,128)}, f32[2,512,256]{2,1,0:T(8,128)}) custom-call(f32[2,4,2,2,512,128]{5,4,3,2,1,0:T(8,128)} %table.1.table_ref, f32[2,512,256]{2,1,0:T(8,128)} %copy-done.1), custom_call_target="tpu_custom_call" | custom-call | flops 40000000 | bytes 14000000 | tf_op jit(solution)/shard_map/source_step/pallas_call | solution.py:436
  74.4 0.0 collective-permute-done.state_ref
  74.4 0.0 copy-start
  74.4 1.0 copy-done
  75.4 13.3 %final_step.1 = (f32[1,2,2,512,256]{4,3,2,1,0:T(8,128)}, f32[16,264,128]{2,1,0:T(8,128)}) custom-call(s32[1,16]{1,0:T(1,128)} %owners_ref.1, s32[1,16]{1,0:T(1,128)} %slots_ref.1, f32[2,4,2,2,512,128]{5,4,3,2,1,0:T(8,128)} %table.1.table_ref, f32[2,512,256]{2,1,0:T(8,128)} %copy-done, f32[1,2,512,256]{3,2,1,0:T(8,128)} %get-tuple-element.13.steps_ref, ...), custom_call_target="tpu_custom_call" | custom-call | flops 40000000 | bytes 14000000 | tf_op jit(solution)/shard_map/final_step/pallas_call | solution.py:462
  88.7 55.1 %volume.1 = f32[8,128,128]{2,1,0:T(8,128)} custom-call(f32[16,264,128]{2,1,0:T(8,128)} %get-tuple-element.16.buffer_ref), custom_call_target="tpu_custom_call" | custom-call | tf_op jit(solution)/shard_map/volume/pallas_call | solution.py:471
  143.8 1.9 %copy.12 = f32[8,128,128]{2,1,0:T(8,128)} copy(f32[8,128,128]{2,1,0:T(8,128)} %volume.1) | data formatting | bytes 1048576
Async XLA Ops:
  44.5 17.9 %collective-permute-start.1 = (f32[2,512,256]{2,1,0:T(8,128)}, f32[2,512,256]{2,1,0:T(8,128)S(1)}, u32[]{:S(2)}, u32[]{:S(2)}) collective-permute-start(f32[2,512,256]{2,1,0:T(8,128)} %get-tuple-element.11.end_ref), channel_id=1, source_target_pairs={{0,1},{1,2},{2,3},{3,4},{4,5},{5,6},{6,7},{7,8},{8,9},{9,10},{10,1... | collective-permute-start | bytes 3145736 | tf_op jit(solution)/shard_map/ppermute | solution.py:25
  60.0 14.4 %collective-permute-start = (f32[2,512,256]{2,1,0:T(8,128)}, f32[2,512,256]{2,1,0:T(8,128)S(1)}, u32[]{:S(2)}, u32[]{:S(2)}) collective-permute-start(f32[2,512,256]{2,1,0:T(8,128)} %get-tuple-element.12), channel_id=1, source_target_pairs={{0,1},{1,2},{2,3},{3,4},{4,5},{5,6},{6,7},{7,8},{8,9},{9,10},{10,1... | collective-permute-start | bytes 3145736 | tf_op jit(solution)/shard_map/ppermute | solution.py:25
  62.3 1.0 copy-start.1
  74.4 1.0 copy-start

commit v3 on v2

--- a/solution.py
+++ b/solution.py
@@ -349,26 +349,35 @@
         copy.wait_send()
 
 
-def volume_kernel(buffer_ref, volume_ref, received, send_sem, recv_sem):
+def volume_kernel(
+    buffer_ref, volume_ref, across, landed, far, near, send_sem, far_sem, near_sem, cross_sem
+):
     me = lax.axis_index("depth")
     peers = buffer_ref.shape[0]
+    half = peers // 2
     tile = volume_ref.shape[1]
     step = 32
-    meet([(me + d) % peers for d in range(1, peers)])
-    copies = []
-    for d in range(1, peers):
-        to = (me + d) % peers
-        copy = remote(buffer_ref.at[to], received.at[d], send_sem.at[d], recv_sem.at[d], to)
+    side = me // half
+    pos = me % half
+    mirror = (me + half) % peers
+    mates = [side * half + (pos + d) % half for d in range(1, half)]
+    meet(mates + [mirror])
+    far_copies, near_copies = [], []
+    for d, mate in enumerate(mates, 1):
+        copy = remote(
+            buffer_ref.at[(mate + half) % peers], far.at[d], send_sem.at[d], far_sem.at[d], mate
+        )
         copy.start()
-        copies.append(copy)
+        far_copies.append(copy)
 
     def clear(m, _):
         volume_ref[m] = jnp.zeros((tile, LANES), jnp.float32)
+        across[m] = jnp.zeros((tile, LANES), jnp.float32)
         return 0
 
     lax.fori_loop(0, volume_ref.shape[0], clear, 0)
 
-    def add_from(ref, block):
+    def add_from(ref, block, total):
         for c in range(CAP):
             slot = ref[block, CAP * tile + c : CAP * tile + c + 1, :]
             slot = jnp.broadcast_to(slot, (8, LANES))
@@ -379,16 +388,35 @@
                 piece = ref[block, pl.ds(c * tile + r0, step), :]
                 for m in range(IMG_SLOTS):
                     here = pl.ds(r0, step)
-                    volume_ref[m, here, :] += jnp.where(slot == m, piece, 0.0)
+                    total[m, here, :] += jnp.where(slot == m, piece, 0.0)
                 return 0
 
             lax.fori_loop(0, tile // step, body, 0)
 
-    add_from(buffer_ref, me)
-    for d, copy in enumerate(copies, 1):
+    add_from(buffer_ref, mirror, across)
+    for d, copy in enumerate(far_copies, 1):
         copy.wait_recv()
-        add_from(received, d)
-    for copy in copies:
+        add_from(far, d, across)
+    add_from(buffer_ref, me, volume_ref)
+    cross = remote(across, landed, send_sem.at[0], cross_sem, mirror)
+    cross.start()
+    for d, mate in enumerate(mates, 1):
+        copy = remote(
+            buffer_ref.at[mate], near.at[d], send_sem.at[half + d], near_sem.at[d], mate
+        )
+        copy.start()
+        near_copies.append(copy)
+    for d, copy in enumerate(near_copies, 1):
+        copy.wait_recv()
+        add_from(near, d, volume_ref)
+    cross.wait_recv()
+
+    def join(m, _):
+        volume_ref[m] = volume_ref[m] + landed[m]
+        return 0
+
+    lax.fori_loop(0, volume_ref.shape[0], join, 0)
+    for copy in far_copies + near_copies + [cross]:
         copy.wait_send()
 
 
@@ -474,9 +502,14 @@
         in_specs=specs(VMEM),
         out_specs=specs(VMEM)[0],
         scratch_shapes=[
-            VMEM((peers, block_rows, LANES), f32),
+            VMEM((IMG_SLOTS, tile, LANES), f32),
+            VMEM((IMG_SLOTS, tile, LANES), f32),
+            VMEM((peers // 2, block_rows, LANES), f32),
+            VMEM((peers // 2, block_rows, LANES), f32),
             pltpu.SemaphoreType.DMA((peers,)),
-            pltpu.SemaphoreType.DMA((peers,)),
+            pltpu.SemaphoreType.DMA((peers // 2,)),
+            pltpu.SemaphoreType.DMA((peers // 2,)),
+            pltpu.SemaphoreType.DMA,
         ],
         compiler_params=pltpu.CompilerParams(collective_id=1, has_side_effects=True),
         name="volume",

time: 146 us -> 136 us (0.932)
  Pallas kernels: 134 us -> 123 us
    pallas_call x1, Pallas kernels: 55.1 us -> 44.2 us  [local(): pl.pallas_call(volume_kernel, out_shape=shape(IMG_SLOTS, tile, LANES), in...]
  transfers between devices with their start and end apart: 2 -> 2, of which waited for: 0 -> 0; matrix products, arithmetic and copies ran while one was open for 0% -> 0% of each run, Pallas kernels for 16% -> 17%
where the time goes in v3:
time: 136 us; the launch traced here: 135 us
  Pallas kernels  123 us (90%)
  starting transfers between devices  5.98 us (4%)
  local copies, waits for them, and re-layouts  5.16 us (4%)
    pallas_call x1, Pallas kernels, local(): pl.pallas_call(volume_kernel, out_shape=shape(IMG_SLOTS, tile, LANES), in...  44.2 us
    pallas_call x2, Pallas kernels, source_call(): pl.pallas_call(source_kernel, grid=(1,), out_shape=(shape(max(steps - 1,...  22 us
    pallas_call x1, Pallas kernels, local(): pl.pallas_call(gather_kernel, out_shape=shape(peers, *vel_tiles.shape), i...  20.4 us
    pallas_call x1, Pallas kernels, local(): pl.pallas_call(final_kernel, out_shape=(shape(1, 2, 2, rows, columns), sh...  13.3 us
    pallas_call x1, Pallas kernels, local(): pl.pallas_call(receiver_kernel, grid=(1,), out_shape=(shape(2, rows, colu...  11.9 us
    pallas_call x1, Pallas kernels, local(): pl.pallas_call(table_kernel, out_shape=shape(steps, degrees, 2, halves, r...  11.1 us
    ppermute x2, starting transfers between devices, from_behind(): return lax.ppermute(shard, axis, pairs)  5.98 us
    unnamed x6, local copies, waits for them, and re-layouts  5.16 us
  transfers between devices with their start and end apart: 2, of which 0 were waited for; matrix products, arithmetic and copies ran while one was open for 0% of the time, Pallas kernels for 17%

profile of v3, /device:TPU:13, one launch (start us, length us, event | category | flops | bytes accessed | tf_op | source)
XLA Modules:
  0.0 134.8 jit_solution(1898101602528686768)
XLA Ops:
  0.6 1.4 %copy.10.ids_ref = s32[1,2,4,2]{3,2,1,0:T(4,128)} copy(s32[1,2,4,2]{2,3,1,0:T(2,128)} %param.10) | data formatting | bytes 128 | tf_op args[2]
  2.0 20.4 %gather.1 = f32[16,2,128,128]{3,2,1,0:T(8,128)} custom-call(f32[2,128,128]{2,1,0:T(8,128)} %own_ref.1), custom_call_target="tpu_custom_call" | custom-call | tf_op jit(solution)/shard_map/gather/pallas_call | solution.py:441
  22.4 11.1 %table.1.table_ref = f32[2,4,2,2,512,128]{5,4,3,2,1,0:T(8,128)} custom-call(s32[1,2,4,2]{3,2,1,0:T(4,128)} %copy.10.ids_ref, s32[1,2]{1,0:T(1,128)} %orders_ref.1, f32[3]{0:T(128)} %term_ref.1, f32[4]{0:T(128)} %rates_ref.1, f32[32,128,128]{2,1,0:T(8,128)} %bitcast.1), custom_call_target="tpu_custom_call" | custom-call | tf_op jit(solution)/shard_map/table/pallas_call | solution.py:450
  33.5 11.0 %source_step.2 = (f32[1,2,512,256]{3,2,1,0:T(8,128)}, f32[2,512,256]{2,1,0:T(8,128)}) custom-call(f32[2,4,2,2,512,128]{5,4,3,2,1,0:T(8,128)} %table.1.table_ref, f32[1,2,2,512,256]{4,3,2,1,0:T(8,128)} %state_ref.3), custom_call_target="tpu_custom_call" | custom-call | flops 40000000 | bytes 14000000 | tf_op jit(solution)/shard_map/source_step/pallas_call | solution.py:464
  44.5 3.7 %collective-permute-start.1 = (f32[2,512,256]{2,1,0:T(8,128)}, f32[2,512,256]{2,1,0:T(8,128)S(1)}, u32[]{:S(2)}, u32[]{:S(2)}) collective-permute-start(f32[2,512,256]{2,1,0:T(8,128)} %get-tuple-element.11.end_ref), channel_id=1, source_target_pairs={{0,1},{1,2},{2,3},{3,4},{4,5},{5,6},{6,7},{7,8},{8,9},{9,10},{10,1... | collective-permute-start | bytes 3145736 | tf_op jit(solution)/shard_map/ppermute | solution.py:25
  48.1 11.9 %receiver_step.1 = (f32[2,512,256]{2,1,0:T(8,128)}, f32[2,2,512,128]{3,2,1,0:T(8,128)}) custom-call(f32[2,4,2,2,512,128]{5,4,3,2,1,0:T(8,128)} %table.1.table_ref, f32[1,2,2,512,256]{4,3,2,1,0:T(8,128)} %state_ref.3, f32[1,2,512,256]{3,2,1,0:T(8,128)} %get-tuple-element.10.steps_ref, f32[2,512,256]{2,1,0:T(8,128)} %get-tuple-element.11.end_ref), custom_call_target="tpu_custom_call" | custom-call | flops 40000000 | bytes 14000000 | tf_op jit(solution)/shard_map/receiver_step/pallas_call | solution.py:477
  60.0 2.3 %collective-permute-start = (f32[2,512,256]{2,1,0:T(8,128)}, f32[2,512,256]{2,1,0:T(8,128)S(1)}, u32[]{:S(2)}, u32[]{:S(2)}) collective-permute-start(f32[2,512,256]{2,1,0:T(8,128)} %get-tuple-element.12), channel_id=1, source_target_pairs={{0,1},{1,2},{2,3},{3,4},{4,5},{5,6},{6,7},{7,8},{8,9},{9,10},{10,1... | collective-permute-start | bytes 3145736 | tf_op jit(solution)/shard_map/ppermute | solution.py:25
  62.3 0.0 collective-permute-done.1.state_ref
  62.3 0.0 copy-start.1
  62.3 1.0 copy-done.1
  63.3 11.1 %source_step.3 = (f32[1,2,512,256]{3,2,1,0:T(8,128)}, f32[2,512,256]{2,1,0:T(8,128)}) custom-call(f32[2,4,2,2,512,128]{5,4,3,2,1,0:T(8,128)} %table.1.table_ref, f32[2,512,256]{2,1,0:T(8,128)} %copy-done.1), custom_call_target="tpu_custom_call" | custom-call | flops 40000000 | bytes 14000000 | tf_op jit(solution)/shard_map/source_step/pallas_call | solution.py:464
  74.4 0.0 collective-permute-done.state_ref
  74.4 0.0 copy-start
  74.4 1.0 copy-done
  75.4 13.3 %final_step.1 = (f32[1,2,2,512,256]{4,3,2,1,0:T(8,128)}, f32[16,264,128]{2,1,0:T(8,128)}) custom-call(s32[1,16]{1,0:T(1,128)} %owners_ref.1, s32[1,16]{1,0:T(1,128)} %slots_ref.1, f32[2,4,2,2,512,128]{5,4,3,2,1,0:T(8,128)} %table.1.table_ref, f32[2,512,256]{2,1,0:T(8,128)} %copy-done, f32[1,2,512,256]{3,2,1,0:T(8,128)} %get-tuple-element.13.steps_ref, ...), custom_call_target="tpu_custom_call" | custom-call | flops 40000000 | bytes 14000000 | tf_op jit(solution)/shard_map/final_step/pallas_call | solution.py:490
  88.7 44.2 %volume.1 = f32[8,128,128]{2,1,0:T(8,128)} custom-call(f32[16,264,128]{2,1,0:T(8,128)} %get-tuple-element.16.buffer_ref), custom_call_target="tpu_custom_call" | custom-call | tf_op jit(solution)/shard_map/volume/pallas_call | solution.py:499
  132.9 1.9 %copy.12 = f32[8,128,128]{2,1,0:T(8,128)} copy(f32[8,128,128]{2,1,0:T(8,128)} %volume.1) | data formatting | bytes 1048576
Async XLA Ops:
  44.5 17.9 %collective-permute-start.1 = (f32[2,512,256]{2,1,0:T(8,128)}, f32[2,512,256]{2,1,0:T(8,128)S(1)}, u32[]{:S(2)}, u32[]{:S(2)}) collective-permute-start(f32[2,512,256]{2,1,0:T(8,128)} %get-tuple-element.11.end_ref), channel_id=1, source_target_pairs={{0,1},{1,2},{2,3},{3,4},{4,5},{5,6},{6,7},{7,8},{8,9},{9,10},{10,1... | collective-permute-start | bytes 3145736 | tf_op jit(solution)/shard_map/ppermute | solution.py:25
  60.0 14.4 %collective-permute-start = (f32[2,512,256]{2,1,0:T(8,128)}, f32[2,512,256]{2,1,0:T(8,128)S(1)}, u32[]{:S(2)}, u32[]{:S(2)}) collective-permute-start(f32[2,512,256]{2,1,0:T(8,128)} %get-tuple-element.12), channel_id=1, source_target_pairs={{0,1},{1,2},{2,3},{3,4},{4,5},{5,6},{6,7},{7,8},{8,9},{9,10},{10,1... | collective-permute-start | bytes 3145736 | tf_op jit(solution)/shard_map/ppermute | solution.py:25
  62.3 1.0 copy-start.1
  74.4 1.0 copy-start

commit v4 on v3

--- a/solution.py
+++ b/solution.py
@@ -174,7 +174,7 @@
     lax.fori_loop(0, chunks, first, 0, unroll=2)
     lax.fori_loop(0, chunks, second, 0, unroll=2)
     copy.wait()
-    lax.fori_loop(0, chunks, third, 0)
+    lax.fori_loop(0, chunks, third, 0, unroll=2)
 
 
 def source_kernel(table_ref, state_ref, out_ref, end_ref, p0, p1, p2, table, sems):

time: 136 us -> 132 us (0.971)
  Pallas kernels: 123 us -> 118 us
    pallas_call x2, Pallas kernels: 22 us -> 19.5 us  [source_call(): pl.pallas_call(source_kernel, grid=(1,), out_shape=(shape(max(steps - 1,...]
  transfers between devices with their start and end apart: 2 -> 2, of which waited for: 0 -> 1; matrix products, arithmetic and copies ran while one was open for 0% -> 0% of each run, Pallas kernels for 17% -> 16%
where the time goes in v4:
time: 132 us; the launch traced here: 131 us
  Pallas kernels  118 us (89%)
  starting transfers between devices  5.98 us (5%)
  local copies, waits for them, and re-layouts  5.17 us (4%)
    pallas_call x1, Pallas kernels, local(): pl.pallas_call(volume_kernel, out_shape=shape(IMG_SLOTS, tile, LANES), in...  44.3 us
    pallas_call x1, Pallas kernels, local(): pl.pallas_call(gather_kernel, out_shape=shape(peers, *vel_tiles.shape), i...  20.4 us
    pallas_call x2, Pallas kernels, source_call(): pl.pallas_call(source_kernel, grid=(1,), out_shape=(shape(max(steps - 1,...  19.5 us
    pallas_call x1, Pallas kernels, local(): pl.pallas_call(final_kernel, out_shape=(shape(1, 2, 2, rows, columns), sh...  12 us
    pallas_call x1, Pallas kernels, local(): pl.pallas_call(table_kernel, out_shape=shape(steps, degrees, 2, halves, r...  11.1 us
    pallas_call x1, Pallas kernels, local(): pl.pallas_call(receiver_kernel, grid=(1,), out_shape=(shape(2, rows, colu...  10.6 us
    ppermute x2, starting transfers between devices, from_behind(): return lax.ppermute(shard, axis, pairs)  5.98 us
    unnamed x6, local copies, waits for them, and re-layouts  5.17 us
  transfers between devices with their start and end apart: 2, of which 1 were waited for; matrix products, arithmetic and copies ran while one was open for 0% of the time, Pallas kernels for 16%

profile of v4, /device:TPU:13, one launch (start us, length us, event | category | flops | bytes accessed | tf_op | source)
XLA Modules:
  0.0 131.0 jit_solution(3958982143279942070)
XLA Ops:
  0.6 1.4 %copy.10.ids_ref = s32[1,2,4,2]{3,2,1,0:T(4,128)} copy(s32[1,2,4,2]{2,3,1,0:T(2,128)} %param.10) | data formatting | bytes 128 | tf_op args[2]
  2.0 20.4 %gather.1 = f32[16,2,128,128]{3,2,1,0:T(8,128)} custom-call(f32[2,128,128]{2,1,0:T(8,128)} %own_ref.1), custom_call_target="tpu_custom_call" | custom-call | tf_op jit(solution)/shard_map/gather/pallas_call | solution.py:441
  22.4 11.1 %table.1.table_ref = f32[2,4,2,2,512,128]{5,4,3,2,1,0:T(8,128)} custom-call(s32[1,2,4,2]{3,2,1,0:T(4,128)} %copy.10.ids_ref, s32[1,2]{1,0:T(1,128)} %orders_ref.1, f32[3]{0:T(128)} %term_ref.1, f32[4]{0:T(128)} %rates_ref.1, f32[32,128,128]{2,1,0:T(8,128)} %bitcast.1), custom_call_target="tpu_custom_call" | custom-call | tf_op jit(solution)/shard_map/table/pallas_call | solution.py:450
  33.5 9.7 %source_step.2 = (f32[1,2,512,256]{3,2,1,0:T(8,128)}, f32[2,512,256]{2,1,0:T(8,128)}) custom-call(f32[2,4,2,2,512,128]{5,4,3,2,1,0:T(8,128)} %table.1.table_ref, f32[1,2,2,512,256]{4,3,2,1,0:T(8,128)} %state_ref.3), custom_call_target="tpu_custom_call" | custom-call | flops 40000000 | bytes 14000000 | tf_op jit(solution)/shard_map/source_step/pallas_call | solution.py:464
  43.2 3.7 %collective-permute-start.1 = (f32[2,512,256]{2,1,0:T(8,128)}, f32[2,512,256]{2,1,0:T(8,128)S(1)}, u32[]{:S(2)}, u32[]{:S(2)}) collective-permute-start(f32[2,512,256]{2,1,0:T(8,128)} %get-tuple-element.11.end_ref), channel_id=1, source_target_pairs={{0,1},{1,2},{2,3},{3,4},{4,5},{5,6},{6,7},{7,8},{8,9},{9,10},{10,1... | collective-permute-start | bytes 3145736 | tf_op jit(solution)/shard_map/ppermute | solution.py:25
  46.9 10.6 %receiver_step.1 = (f32[2,512,256]{2,1,0:T(8,128)}, f32[2,2,512,128]{3,2,1,0:T(8,128)}) custom-call(f32[2,4,2,2,512,128]{5,4,3,2,1,0:T(8,128)} %table.1.table_ref, f32[1,2,2,512,256]{4,3,2,1,0:T(8,128)} %state_ref.3, f32[1,2,512,256]{3,2,1,0:T(8,128)} %get-tuple-element.10.steps_ref, f32[2,512,256]{2,1,0:T(8,128)} %get-tuple-element.11.end_ref), custom_call_target="tpu_custom_call" | custom-call | flops 40000000 | bytes 14000000 | tf_op jit(solution)/shard_map/receiver_step/pallas_call | solution.py:477
  57.5 2.3 %collective-permute-start = (f32[2,512,256]{2,1,0:T(8,128)}, f32[2,512,256]{2,1,0:T(8,128)S(1)}, u32[]{:S(2)}, u32[]{:S(2)}) collective-permute-start(f32[2,512,256]{2,1,0:T(8,128)} %get-tuple-element.12), channel_id=1, source_target_pairs={{0,1},{1,2},{2,3},{3,4},{4,5},{5,6},{6,7},{7,8},{8,9},{9,10},{10,1... | collective-permute-start | bytes 3145736 | tf_op jit(solution)/shard_map/ppermute | solution.py:25
  59.8 0.0 collective-permute-done.1.state_ref
  59.8 0.0 copy-start.1
  59.8 1.0 copy-done.1
  60.7 9.8 %source_step.3 = (f32[1,2,512,256]{3,2,1,0:T(8,128)}, f32[2,512,256]{2,1,0:T(8,128)}) custom-call(f32[2,4,2,2,512,128]{5,4,3,2,1,0:T(8,128)} %table.1.table_ref, f32[2,512,256]{2,1,0:T(8,128)} %copy-done.1), custom_call_target="tpu_custom_call" | custom-call | flops 40000000 | bytes 14000000 | tf_op jit(solution)/shard_map/source_step/pallas_call | solution.py:464
  70.6 1.2 collective-permute-done.state_ref
  71.8 0.0 copy-start
  71.8 1.0 copy-done
  72.8 12.0 %final_step.1 = (f32[1,2,2,512,256]{4,3,2,1,0:T(8,128)}, f32[16,264,128]{2,1,0:T(8,128)}) custom-call(s32[1,16]{1,0:T(1,128)} %owners_ref.1, s32[1,16]{1,0:T(1,128)} %slots_ref.1, f32[2,4,2,2,512,128]{5,4,3,2,1,0:T(8,128)} %table.1.table_ref, f32[2,512,256]{2,1,0:T(8,128)} %copy-done, f32[1,2,512,256]{3,2,1,0:T(8,128)} %get-tuple-element.13.steps_ref, ...), custom_call_target="tpu_custom_call" | custom-call | flops 40000000 | bytes 14000000 | tf_op jit(solution)/shard_map/final_step/pallas_call | solution.py:490
  84.8 44.3 %volume.1 = f32[8,128,128]{2,1,0:T(8,128)} custom-call(f32[16,264,128]{2,1,0:T(8,128)} %get-tuple-element.16.buffer_ref), custom_call_target="tpu_custom_call" | custom-call | tf_op jit(solution)/shard_map/volume/pallas_call | solution.py:499
  129.1 1.9 %copy.12 = f32[8,128,128]{2,1,0:T(8,128)} copy(f32[8,128,128]{2,1,0:T(8,128)} %volume.1) | data formatting | bytes 1048576
Async XLA Ops:
  43.2 16.6 %collective-permute-start.1 = (f32[2,512,256]{2,1,0:T(8,128)}, f32[2,512,256]{2,1,0:T(8,128)S(1)}, u32[]{:S(2)}, u32[]{:S(2)}) collective-permute-start(f32[2,512,256]{2,1,0:T(8,128)} %get-tuple-element.11.end_ref), channel_id=1, source_target_pairs={{0,1},{1,2},{2,3},{3,4},{4,5},{5,6},{6,7},{7,8},{8,9},{9,10},{10,1... | collective-permute-start | bytes 3145736 | tf_op jit(solution)/shard_map/ppermute | solution.py:25
  57.5 14.3 %collective-permute-start = (f32[2,512,256]{2,1,0:T(8,128)}, f32[2,512,256]{2,1,0:T(8,128)S(1)}, u32[]{:S(2)}, u32[]{:S(2)}) collective-permute-start(f32[2,512,256]{2,1,0:T(8,128)} %get-tuple-element.12), channel_id=1, source_target_pairs={{0,1},{1,2},{2,3},{3,4},{4,5},{5,6},{6,7},{7,8},{8,9},{9,10},{10,1... | collective-permute-start | bytes 3145736 | tf_op jit(solution)/shard_map/ppermute | solution.py:25
  59.8 1.0 copy-start.1
  71.8 1.0 copy-start
